TPU v7x, 32 devices: a whole 2x2x4 slice. The times are simulated.
32 devices in a mesh: band: 8 (over z, x), dom: 4 (over y, core).
Axes of the slice: x: 2, y: 2, z: 4, core: 2. Of those that a mesh axis runs over, the one named last changes fastest.
Arguments:
- orbitals: bfloat16 [512, 16, 2048], P('band', 'dom'), may hold values from -6 to 6
- potential: float32 [16, 2048], P('dom'), may hold values from 0 to 2
- bounds: float32 [2], replicated, may hold values from 1 to 10, as said below
Outputs:
- rotated: bfloat16 [512, 16, 2048], P('band', 'dom')
- projected: float32 [512, 512], replicated
Inputs may be any that keep to these rules, and one draw needn't show every extreme that they name: bounds[0] lies in 1 to 2 and bounds[1] in 8.5 to 10, above the whole spectrum of H.
All inputs are finite; a program needn't handle non-finite values.
Results may differ from a plain program's by a relative error of at most 0.006.
Values may be sent and summed in bfloat16 or wider, within the bound.
A program may use at most 128 MiB of HBM per device.

v0:
```python
import jax
import jax.numpy as jnp
from jax import lax
from jax.sharding import PartitionSpec as P

BANDS = 512
GRID_Y = 64
GRID_Z = 32
DEG = 8
NS_STEPS = 8


def padded(cells, sides, width):
    for axis, dim in sides:
        count = lax.axis_size(axis)
        head = lax.slice_in_dim(cells, 0, width, axis=dim)
        tail = lax.slice_in_dim(cells, cells.shape[dim] - width, cells.shape[dim], axis=dim)
        cells = jnp.concatenate(
            [
                lax.ppermute(tail, axis, [(i, (i + 1) % count) for i in range(count)]),
                cells,
                lax.ppermute(head, axis, [((i + 1) % count, i) for i in range(count)]),
            ],
            axis=dim,
        )
    return cells


def planes(field):
    return field.reshape(field.shape[0], field.shape[1], GRID_Y, GRID_Z)


def flatten(field):
    return field.reshape(field.shape[0], field.shape[1], GRID_Y * GRID_Z)


def stencil(widened, pot_planes):
    middle = widened[:, 1:-1]
    beside = widened[:, 2:] + widened[:, :-2]
    beside = beside + jnp.roll(middle, -1, 2) + jnp.roll(middle, 1, 2)
    beside = beside + jnp.roll(middle, -1, 3) + jnp.roll(middle, 1, 3)
    return -0.5 * (beside - 6.0 * middle) + pot_planes * middle


def slab_filter(start, potential, half_width, centre):
    slab = start.shape[1]
    pot_inner = potential.reshape(slab, GRID_Y, GRID_Z)

    def apply_once(field):
        widened = padded(field, (("dom", 1),), 1)
        return flatten(stencil(planes(widened), pot_inner))

    earlier = start
    current = (apply_once(start) - centre * start) / half_width
    for repeat in range(DEG - 1):
        following = 2.0 * (apply_once(current) - centre * current) / half_width - earlier
        earlier = current
        current = following
    applied = apply_once(current)
    return (current, applied)


def gram_pair(point_filt, point_applied, cell_volume):
    contract = (((1,), (1,)), ((), ()))
    correlation_part = (
        lax.dot_general(point_filt, point_filt, contract, preferred_element_type=jnp.float32)
        * cell_volume
    )
    hamil_part = (
        lax.dot_general(point_filt, point_applied, contract, preferred_element_type=jnp.float32)
        * cell_volume
    )
    return lax.psum((correlation_part, hamil_part), ("band", "dom"))


def body(orbitals, potential, bounds):
    local_bands = orbitals.shape[0]
    slab = orbitals.shape[1]
    dom_count = lax.axis_size("dom")
    lower_cut = bounds[0]
    upper_cut = bounds[1]
    half_width = (upper_cut - lower_cut) / 2.0
    centre = (upper_cut + lower_cut) / 2.0
    slab_points = slab * GRID_Y * GRID_Z
    cell_volume = 1.0 / (slab_points * dom_count)
    start = orbitals.astype(jnp.float32)
    current, applied = slab_filter(start, potential, half_width, centre)
    filt_local = current.astype(jnp.bfloat16).reshape(local_bands, slab_points)
    applied_local = applied.astype(jnp.bfloat16).reshape(local_bands, slab_points)
    point_filt, point_applied = (
        lax.all_to_all(filt_local, "band", split_axis=1, concat_axis=0, tiled=True),
        lax.all_to_all(applied_local, "band", split_axis=1, concat_axis=0, tiled=True),
    )
    correlation, hamil_sub = gram_pair(point_filt, point_applied, cell_volume)
    scale = jnp.sqrt(jnp.sum(correlation * correlation) + 1e-06)
    high = lax.Precision.HIGHEST
    identity = jnp.eye(BANDS, dtype=jnp.float32)
    scaled = correlation / scale
    inverse = identity
    for repeat in range(NS_STEPS):
        factor = 1.5 * identity - 0.5 * jnp.dot(inverse, scaled, precision=high)
        scaled = jnp.dot(factor, scaled, precision=high)
        inverse = jnp.dot(factor, inverse, precision=high)
    transform = inverse / jnp.sqrt(scale)
    projected = jnp.dot(jnp.dot(transform.T, hamil_sub, precision=high), transform, precision=high)
    point_rotated = jnp.dot(transform.T, point_filt.astype(jnp.float32), precision=high).astype(
        jnp.bfloat16
    )
    band_rotated = lax.all_to_all(point_rotated, "band", split_axis=0, concat_axis=1, tiled=True)
    return (band_rotated.reshape(local_bands, slab, GRID_Y * GRID_Z), projected)


def solution(mesh):
    return jax.shard_map(
        body,
        mesh=mesh,
        in_specs=(P("band", "dom", None), P("dom", None), P()),
        out_specs=(P("band", "dom", None), P()),
        check_vma=False,
    )
```

profile of v0, /device:TPU:0, one launch (start us, length us, event | category | flops | bytes accessed | tf_op | source)
XLA Modules:
  0.0 625.8 jit_solution(11283899963984443685)
XLA Ops:
  22.4 5.1 collective-permute-done.1
  39.3 5.6 fusion.63
  53.6 11.0 %collective-permute-done.3 = f32[64,1,2048]{2,0,1:T(8,128)} collective-permute-done((f32[64,1,2048]{2,0,1:T(8,128)}, f32[64,1,2048]{2,0,1:T(8,128)}, u32[]{:S(2)}, u32[]{:S(2)}) %collective-permute-start.3) | collective-permute-done | bytes 524320 | tf_op jit(solution)/shard_map/ppermute | solution.py:22
  77.3 7.8 %fusion.56 = f32[64,4,64,32]{0,3,2,1:T(8,128)} fusion(f32[64,6,64,32]{0,3,2,1:T(8,128)S(1)} %bitcast.143, f32[64,4,1,32]{0,3,2,1:T(8,128)S(1)} %get-tuple-element.67, f32[64,4,63,32]{0,3,2,1:T(8,128)} %get-tuple-element.69, f32[64,4,63,32]{0,3,2,1:T(8,128)} %get-tuple-element.68, f32[64,4,1,32]{0,3,2,1:T(8,128)S(1)} %get-tuple-element.66, ...), kind=kLoop, calls=%fused_computation.73 | loop fusion | flops 7340032 | bytes 16809984 | tf_op jit(solution)/shard_map/add | solution.py:42
  93.7 11.2 %collective-permute-done.5 = f32[64,1,2048]{2,0,1:T(8,128)S(1)} collective-permute-done((f32[64,1,2048]{2,0,1:T(8,128)S(1)}, f32[64,1,2048]{2,0,1:T(8,128)S(1)}, u32[]{:S(2)}, u32[]{:S(2)}) %collective-permute-start.5) | collective-permute-done | bytes 524320 | tf_op jit(solution)/shard_map/ppermute | solution.py:22
  115.9 9.9 %fusion.49 = f32[64,4,64,32]{0,3,2,1:T(8,128)} fusion(f32[64,6,64,32]{0,3,2,1:T(8,128)S(1)} %bitcast.148, f32[64,4,1,32]{0,3,2,1:T(8,128)S(1)} %get-tuple-element.59, f32[64,4,63,32]{0,3,2,1:T(8,128)} %get-tuple-element.61, f32[64,4,63,32]{0,3,2,1:T(8,128)} %get-tuple-element.60, f32[64,4,1,32]{0,3,2,1:T(8,128)S(1)} %get-tuple-element.58, ...), kind=kLoop, calls=%fused_computation.65 | loop fusion | flops 7340032 | bytes 16809984 | tf_op jit(solution)/shard_map/add | solution.py:42
  133.5 11.4 %collective-permute-done.7 = f32[64,1,2048]{2,0,1:T(8,128)S(1)} collective-permute-done((f32[64,1,2048]{2,0,1:T(8,128)S(1)}, f32[64,1,2048]{2,0,1:T(8,128)S(1)}, u32[]{:S(2)}, u32[]{:S(2)}) %collective-permute-start.7) | collective-permute-done | bytes 524320 | tf_op jit(solution)/shard_map/ppermute | solution.py:22
  148.8 4.4 fusion.113
  156.2 9.9 %fusion.42 = f32[64,4,64,32]{0,3,2,1:T(8,128)} fusion(f32[64,6,64,32]{0,3,2,1:T(8,128)S(1)} %bitcast.153, f32[64,4,1,32]{0,3,2,1:T(8,128)S(1)} %get-tuple-element.51, f32[64,4,63,32]{0,3,2,1:T(8,128)} %get-tuple-element.53, f32[64,4,63,32]{0,3,2,1:T(8,128)} %get-tuple-element.52, f32[64,4,1,32]{0,3,2,1:T(8,128)S(1)} %get-tuple-element.50, ...), kind=kLoop, calls=%fused_computation.57 | loop fusion | flops 7340032 | bytes 16809984 | tf_op jit(solution)/shard_map/add | solution.py:42
  174.1 11.5 %collective-permute-done.9 = f32[64,1,2048]{2,0,1:T(8,128)S(1)} collective-permute-done((f32[64,1,2048]{2,0,1:T(8,128)S(1)}, f32[64,1,2048]{2,0,1:T(8,128)S(1)}, u32[]{:S(2)}, u32[]{:S(2)}) %collective-permute-start.9) | collective-permute-done | bytes 524320 | tf_op jit(solution)/shard_map/ppermute | solution.py:22
  196.5 9.9 %fusion.35 = f32[64,4,64,32]{0,3,2,1:T(8,128)} fusion(f32[64,6,64,32]{0,3,2,1:T(8,128)S(1)} %bitcast.158, f32[64,4,1,32]{0,3,2,1:T(8,128)S(1)} %get-tuple-element.43, f32[64,4,63,32]{0,3,2,1:T(8,128)} %get-tuple-element.45, f32[64,4,63,32]{0,3,2,1:T(8,128)} %get-tuple-element.44, f32[64,4,1,32]{0,3,2,1:T(8,128)S(1)} %get-tuple-element.42, ...), kind=kLoop, calls=%fused_computation.49 | loop fusion | flops 7340032 | bytes 16809984 | tf_op jit(solution)/shard_map/add | solution.py:42
  214.5 11.7 %collective-permute-done.11 = f32[64,1,2048]{2,0,1:T(8,128)S(1)} collective-permute-done((f32[64,1,2048]{2,0,1:T(8,128)S(1)}, f32[64,1,2048]{2,0,1:T(8,128)S(1)}, u32[]{:S(2)}, u32[]{:S(2)}) %collective-permute-start.11) | collective-permute-done | bytes 524320 | tf_op jit(solution)/shard_map/ppermute | solution.py:22
  229.9 4.4 fusion.105
  237.4 9.9 %fusion.28 = f32[64,4,64,32]{0,3,2,1:T(8,128)} fusion(f32[64,6,64,32]{0,3,2,1:T(8,128)S(1)} %bitcast.163, f32[64,4,1,32]{0,3,2,1:T(8,128)S(1)} %get-tuple-element.35, f32[64,4,63,32]{0,3,2,1:T(8,128)} %get-tuple-element.37, f32[64,4,63,32]{0,3,2,1:T(8,128)} %get-tuple-element.36, f32[64,4,1,32]{0,3,2,1:T(8,128)S(1)} %get-tuple-element.34, ...), kind=kLoop, calls=%fused_computation.41 | loop fusion | flops 7340032 | bytes 16809984 | tf_op jit(solution)/shard_map/add | solution.py:42
  255.1 11.7 %collective-permute-done.13 = f32[64,1,2048]{2,0,1:T(8,128)S(1)} collective-permute-done((f32[64,1,2048]{2,0,1:T(8,128)S(1)}, f32[64,1,2048]{2,0,1:T(8,128)S(1)}, u32[]{:S(2)}, u32[]{:S(2)}) %collective-permute-start.13) | collective-permute-done | bytes 524320 | tf_op jit(solution)/shard_map/ppermute | solution.py:22
  277.8 9.9 %fusion.21 = f32[64,4,64,32]{0,3,2,1:T(8,128)} fusion(f32[64,6,64,32]{0,3,2,1:T(8,128)S(1)} %bitcast.168, f32[64,4,1,32]{0,3,2,1:T(8,128)S(1)} %get-tuple-element.27, f32[64,4,63,32]{0,3,2,1:T(8,128)} %get-tuple-element.29, f32[64,4,63,32]{0,3,2,1:T(8,128)} %get-tuple-element.28, f32[64,4,1,32]{0,3,2,1:T(8,128)S(1)} %get-tuple-element.26, ...), kind=kLoop, calls=%fused_computation.33 | loop fusion | flops 7340032 | bytes 16809984 | tf_op jit(solution)/shard_map/add | solution.py:42
  295.7 11.7 %collective-permute-done.15 = f32[64,1,2048]{2,0,1:T(8,128)S(1)} collective-permute-done((f32[64,1,2048]{2,0,1:T(8,128)S(1)}, f32[64,1,2048]{2,0,1:T(8,128)S(1)}, u32[]{:S(2)}, u32[]{:S(2)}) %collective-permute-start.15) | collective-permute-done | bytes 524320 | tf_op jit(solution)/shard_map/ppermute | solution.py:22
  318.6 9.9 %fusion.14 = f32[64,4,64,32]{0,3,2,1:T(8,128)} fusion(f32[64,6,64,32]{0,3,2,1:T(8,128)S(1)} %bitcast.173, f32[64,4,1,32]{0,3,2,1:T(8,128)S(1)} %get-tuple-element.19, f32[64,4,63,32]{0,3,2,1:T(8,128)} %get-tuple-element.21, f32[64,4,63,32]{0,3,2,1:T(8,128)} %get-tuple-element.20, f32[64,4,1,32]{0,3,2,1:T(8,128)S(1)} %get-tuple-element.18, ...), kind=kLoop, calls=%fused_computation.25 | loop fusion | flops 7340032 | bytes 16809984 | tf_op jit(solution)/shard_map/add | solution.py:42
  341.5 5.8 all-to-all-start
  360.7 5.6 fusion.7
  367.9 5.4 all-to-all-done
  379.1 23.8 %all-to-all-done.2 = bf16[64,8,1024]{2,0,1:T(8,128)(2,1)S(1)} async-done(((bf16[64,8,1024]{2,0,1:T(8,128)(2,1)}), bf16[64,8,1024]{2,0,1:T(8,128)(2,1)S(1)}, u32[]{:S(2)}, u32[]{:S(2)}) %all-to-all-start.2) | async-done | bytes 1048608 | tf_op jit(solution)/shard_map/all_to_all | solution.py:92
  404.6 134.3 %all-reduce.3.cloned.1.call-done = (f32[512,512]{1,0:T(8,128)}, f32[512,512]{1,0:T(8,128)}) async-done(((f32[512,512]{1,0:T(8,128)}, f32[512,512]{1,0:T(8,128)}), (f32[512,512]{1,0:T(8,128)}, f32[512,512]{1,0:T(8,128)})) %all-reduce.3.cloned.1.call-update) | async-done | bytes 2097168 | tf_op jit(solution)/shard_map/psum | solution.py:73
  597.9 18.4 %all-to-all-done.1 = bf16[8,64,1024]{2,1,0:T(8,128)(2,1)S(1)} async-done(((bf16[8,64,1024]{2,1,0:T(8,128)(2,1)}), bf16[8,64,1024]{2,1,0:T(8,128)(2,1)S(1)}, u32[]{:S(2)}, u32[]{:S(2)}) %all-to-all-start.1) | async-done | bytes 1048608 | tf_op jit(solution)/shard_map/all_to_all | solution.py:109
  (213 shorter events, 247.5 us)
Async XLA Ops:
  13.5 14.0 %collective-permute-start.1 = (f32[64,1,2048]{2,0,1:T(8,128)}, f32[64,1,2048]{2,0,1:T(8,128)}, u32[]{:S(2)}, u32[]{:S(2)}) collective-permute-start(f32[64,1,2048]{2,0,1:T(8,128)} %copy.12), channel_id=1, source_target_pairs={{1,0},{2,1},{3,2},{0,3},{5,4},{6,5},{7,6},{4,7},{9,8},{10,9},{11,1... | collective-permute-start | bytes 1572872 | tf_op jit(solution)/shard_map/ppermute | solution.py:22
  17.1 12.5 %collective-permute-start = (f32[64,1,2048]{2,0,1:T(8,128)}, f32[64,1,2048]{2,0,1:T(8,128)}, u32[]{:S(2)}, u32[]{:S(2)}) collective-permute-start(f32[64,1,2048]{2,0,1:T(8,128)} %copy.11), channel_id=1, source_target_pairs={{0,1},{1,2},{2,3},{3,0},{4,5},{5,6},{6,7},{7,4},{8,9},{9,10},{10,1... | collective-permute-start | bytes 1572872 | tf_op jit(solution)/shard_map/ppermute | solution.py:20
  51.0 13.6 %collective-permute-start.3 = (f32[64,1,2048]{2,0,1:T(8,128)}, f32[64,1,2048]{2,0,1:T(8,128)}, u32[]{:S(2)}, u32[]{:S(2)}) collective-permute-start(f32[64,1,2048]{2,0,1:T(8,128)} %copy.16), channel_id=1, source_target_pairs={{1,0},{2,1},{3,2},{0,3},{5,4},{6,5},{7,6},{4,7},{9,8},{10,9},{11,1... | collective-permute-start | bytes 1572872 | tf_op jit(solution)/shard_map/ppermute | solution.py:22
  53.6 12.4 %collective-permute-start.2 = (f32[64,1,2048]{2,0,1:T(8,128)}, f32[64,1,2048]{2,0,1:T(8,128)}, u32[]{:S(2)}, u32[]{:S(2)}) collective-permute-start(f32[64,1,2048]{2,0,1:T(8,128)} %copy.15), channel_id=1, source_target_pairs={{0,1},{1,2},{2,3},{3,0},{4,5},{5,6},{6,7},{7,4},{8,9},{9,10},{10,1... | collective-permute-start | bytes 1572872 | tf_op jit(solution)/shard_map/ppermute | solution.py:20
  90.8 14.0 %collective-permute-start.5 = (f32[64,1,2048]{2,0,1:T(8,128)S(1)}, f32[64,1,2048]{2,0,1:T(8,128)S(1)}, u32[]{:S(2)}, u32[]{:S(2)}) collective-permute-start(f32[64,1,2048]{2,0,1:T(8,128)S(1)} %copy.20), channel_id=1, source_target_pairs={{1,0},{2,1},{3,2},{0,3},{5,4},{6,5},{7,6},{4,7},{9,8},{10,9},{11,1... | collective-permute-start | bytes 1572872 | tf_op jit(solution)/shard_map/ppermute | solution.py:22
  93.4 11.9 %collective-permute-start.4 = (f32[64,1,2048]{2,0,1:T(8,128)S(1)}, f32[64,1,2048]{2,0,1:T(8,128)S(1)}, u32[]{:S(2)}, u32[]{:S(2)}) collective-permute-start(f32[64,1,2048]{2,0,1:T(8,128)S(1)} %copy.19), channel_id=1, source_target_pairs={{0,1},{1,2},{2,3},{3,0},{4,5},{5,6},{6,7},{7,4},{8,9},{9,10},{10,1... | collective-permute-start | bytes 1572872 | tf_op jit(solution)/shard_map/ppermute | solution.py:20
  115.9 9.9 %copy-start.17 = (f32[64,4,2048]{0,2,1:T(8,128)S(1)}, f32[64,4,2048]{0,2,1:T(8,128)}, u32[]{:S(2)}) copy-start(f32[64,4,2048]{0,2,1:T(8,128)} %copy-done.15) | copy-start | bytes 6291460
  131.3 13.7 %collective-permute-start.7 = (f32[64,1,2048]{2,0,1:T(8,128)S(1)}, f32[64,1,2048]{2,0,1:T(8,128)S(1)}, u32[]{:S(2)}, u32[]{:S(2)}) collective-permute-start(f32[64,1,2048]{2,0,1:T(8,128)S(1)} %copy.24), channel_id=1, source_target_pairs={{1,0},{2,1},{3,2},{0,3},{5,4},{6,5},{7,6},{4,7},{9,8},{10,9},{11,1... | collective-permute-start | bytes 1572872 | tf_op jit(solution)/shard_map/ppermute | solution.py:22
  133.5 12.1 %collective-permute-start.6 = (f32[64,1,2048]{2,0,1:T(8,128)S(1)}, f32[64,1,2048]{2,0,1:T(8,128)S(1)}, u32[]{:S(2)}, u32[]{:S(2)}) collective-permute-start(f32[64,1,2048]{2,0,1:T(8,128)S(1)} %copy.23), channel_id=1, source_target_pairs={{0,1},{1,2},{2,3},{3,0},{4,5},{5,6},{6,7},{7,4},{8,9},{9,10},{10,1... | collective-permute-start | bytes 1572872 | tf_op jit(solution)/shard_map/ppermute | solution.py:20
  156.2 9.9 %copy-start.7 = (f32[64,4,2048]{0,2,1:T(8,128)S(1)}, f32[64,4,2048]{0,2,1:T(8,128)}, u32[]{:S(2)}) copy-start(f32[64,4,2048]{0,2,1:T(8,128)} %copy-done.6) | copy-start | bytes 6291460
  171.6 13.9 %collective-permute-start.9 = (f32[64,1,2048]{2,0,1:T(8,128)S(1)}, f32[64,1,2048]{2,0,1:T(8,128)S(1)}, u32[]{:S(2)}, u32[]{:S(2)}) collective-permute-start(f32[64,1,2048]{2,0,1:T(8,128)S(1)} %copy.28), channel_id=1, source_target_pairs={{1,0},{2,1},{3,2},{0,3},{5,4},{6,5},{7,6},{4,7},{9,8},{10,9},{11,1... | collective-permute-start | bytes 1572872 | tf_op jit(solution)/shard_map/ppermute | solution.py:22
  173.6 12.3 %collective-permute-start.8 = (f32[64,1,2048]{2,0,1:T(8,128)S(1)}, f32[64,1,2048]{2,0,1:T(8,128)S(1)}, u32[]{:S(2)}, u32[]{:S(2)}) collective-permute-start(f32[64,1,2048]{2,0,1:T(8,128)S(1)} %copy.27), channel_id=1, source_target_pairs={{0,1},{1,2},{2,3},{3,0},{4,5},{5,6},{6,7},{7,4},{8,9},{9,10},{10,1... | collective-permute-start | bytes 1572872 | tf_op jit(solution)/shard_map/ppermute | solution.py:20
  211.9 14.2 %collective-permute-start.11 = (f32[64,1,2048]{2,0,1:T(8,128)S(1)}, f32[64,1,2048]{2,0,1:T(8,128)S(1)}, u32[]{:S(2)}, u32[]{:S(2)}) collective-permute-start(f32[64,1,2048]{2,0,1:T(8,128)S(1)} %copy.32), channel_id=1, source_target_pairs={{1,0},{2,1},{3,2},{0,3},{5,4},{6,5},{7,6},{4,7},{9,8},{10,9},{11,1... | collective-permute-start | bytes 1572872 | tf_op jit(solution)/shard_map/ppermute | solution.py:22
  214.4 12.4 %collective-permute-start.10 = (f32[64,1,2048]{2,0,1:T(8,128)S(1)}, f32[64,1,2048]{2,0,1:T(8,128)S(1)}, u32[]{:S(2)}, u32[]{:S(2)}) collective-permute-start(f32[64,1,2048]{2,0,1:T(8,128)S(1)} %copy.31), channel_id=1, source_target_pairs={{0,1},{1,2},{2,3},{3,0},{4,5},{5,6},{6,7},{7,4},{8,9},{9,10},{10,1... | collective-permute-start | bytes 1572872 | tf_op jit(solution)/shard_map/ppermute | solution.py:20
  252.8 13.9 %collective-permute-start.13 = (f32[64,1,2048]{2,0,1:T(8,128)S(1)}, f32[64,1,2048]{2,0,1:T(8,128)S(1)}, u32[]{:S(2)}, u32[]{:S(2)}) collective-permute-start(f32[64,1,2048]{2,0,1:T(8,128)S(1)} %copy.36), channel_id=1, source_target_pairs={{1,0},{2,1},{3,2},{0,3},{5,4},{6,5},{7,6},{4,7},{9,8},{10,9},{11,1... | collective-permute-start | bytes 1572872 | tf_op jit(solution)/shard_map/ppermute | solution.py:22
  254.8 12.4 %collective-permute-start.12 = (f32[64,1,2048]{2,0,1:T(8,128)S(1)}, f32[64,1,2048]{2,0,1:T(8,128)S(1)}, u32[]{:S(2)}, u32[]{:S(2)}) collective-permute-start(f32[64,1,2048]{2,0,1:T(8,128)S(1)} %copy.35), channel_id=1, source_target_pairs={{0,1},{1,2},{2,3},{3,0},{4,5},{5,6},{6,7},{7,4},{8,9},{9,10},{10,1... | collective-permute-start | bytes 1572872 | tf_op jit(solution)/shard_map/ppermute | solution.py:20
  293.2 14.1 %collective-permute-start.15 = (f32[64,1,2048]{2,0,1:T(8,128)S(1)}, f32[64,1,2048]{2,0,1:T(8,128)S(1)}, u32[]{:S(2)}, u32[]{:S(2)}) collective-permute-start(f32[64,1,2048]{2,0,1:T(8,128)S(1)} %copy.40), channel_id=1, source_target_pairs={{1,0},{2,1},{3,2},{0,3},{5,4},{6,5},{7,6},{4,7},{9,8},{10,9},{11,1... | collective-permute-start | bytes 1572872 | tf_op jit(solution)/shard_map/ppermute | solution.py:22
  295.6 12.4 %collective-permute-start.14 = (f32[64,1,2048]{2,0,1:T(8,128)S(1)}, f32[64,1,2048]{2,0,1:T(8,128)S(1)}, u32[]{:S(2)}, u32[]{:S(2)}) collective-permute-start(f32[64,1,2048]{2,0,1:T(8,128)S(1)} %copy.39), channel_id=1, source_target_pairs={{0,1},{1,2},{2,3},{3,0},{4,5},{5,6},{6,7},{7,4},{8,9},{9,10},{10,1... | collective-permute-start | bytes 1572872 | tf_op jit(solution)/shard_map/ppermute | solution.py:20
  337.1 13.8 %collective-permute-start.17 = (f32[64,1,2048]{2,0,1:T(8,128)}, f32[64,1,2048]{2,0,1:T(8,128)}, u32[]{:S(2)}, u32[]{:S(2)}) collective-permute-start(f32[64,1,2048]{2,0,1:T(8,128)} %copy.46), channel_id=1, source_target_pairs={{1,0},{2,1},{3,2},{0,3},{5,4},{6,5},{7,6},{4,7},{9,8},{10,9},{11,1... | collective-permute-start | bytes 1572872 | tf_op jit(solution)/shard_map/ppermute | solution.py:22
  339.9 12.4 %collective-permute-start.16 = (f32[64,1,2048]{2,0,1:T(8,128)}, f32[64,1,2048]{2,0,1:T(8,128)}, u32[]{:S(2)}, u32[]{:S(2)}) collective-permute-start(f32[64,1,2048]{2,0,1:T(8,128)} %copy.45), channel_id=1, source_target_pairs={{0,1},{1,2},{2,3},{3,0},{4,5},{5,6},{6,7},{7,4},{8,9},{9,10},{10,1... | collective-permute-start | bytes 1572872 | tf_op jit(solution)/shard_map/ppermute | solution.py:20
  341.5 31.8 %all-to-all-start = ((bf16[64,8,1024]{2,0,1:T(8,128)(2,1)}), bf16[64,8,1024]{2,0,1:T(8,128)(2,1)S(1)}, u32[]{:S(2)}, u32[]{:S(2)}) async-start(bf16[64,8,1024]{2,0,1:T(8,128)(2,1)} %copy.43), calls=%async_computation | async-start | bytes 2097152 | tf_op jit(solution)/shard_map/all_to_all | solution.py:91
  373.3 29.6 %all-to-all-start.2 = ((bf16[64,8,1024]{2,0,1:T(8,128)(2,1)}), bf16[64,8,1024]{2,0,1:T(8,128)(2,1)S(1)}, u32[]{:S(2)}, u32[]{:S(2)}) async-start(bf16[64,8,1024]{2,0,1:T(8,128)(2,1)} %copy.49), calls=%async_computation.2 | async-start | bytes 2097152 | tf_op jit(solution)/shard_map/all_to_all | solution.py:92
  376.9 162.0 %all-reduce.3.cloned.1.call-start = ((), (), s32[]{:S(2)}) async-start(), calls=%async_computation.3 | async-start | bytes 4194304 | tf_op jit(solution)/shard_map/psum | solution.py:73
  587.7 28.6 %all-to-all-start.1 = ((bf16[8,64,1024]{2,1,0:T(8,128)(2,1)}), bf16[8,64,1024]{2,1,0:T(8,128)(2,1)S(1)}, u32[]{:S(2)}, u32[]{:S(2)}) async-start(bf16[8,64,1024]{2,1,0:T(8,128)(2,1)} %bitcast.21), calls=%async_computation.1 | async-start | bytes 2097152 | tf_op jit(solution)/shard_map/all_to_all | solution.py:109
  (22 other events, 143.8 us)
Sparse Core Ops, SparseCore 0:
  404.7 134.1 all-reduce.2
where the time goes:
time: 636 us; the launch traced here: 626 us
  waiting for transfers between devices  273 us (43%)
  other arithmetic  129 us (20%)
  local copies, waits for them, and re-layouts  118 us (19%)
  matrix products  54.9 us (9%)
  starting transfers between devices  32.6 us (5%)
  between operations  18.4 us (3%)
    psum x1, waiting for transfers between devices, gram_pair(): return lax.psum((correlation_part, hamil_part), ('band', 'dom'))  134 us
    ppermute x9, waiting for transfers between devices, padded(): lax.ppermute(head, axis, [((i + 1) % count, i) for i in range(count)])  88.7 us
    add x8, other arithmetic, stencil(): return -0.5 * (beside - 6.0 * middle) + pot_planes * middle  72.6 us
    slice x18, local copies, waits for them, and re-layouts, stencil(): beside = beside + jnp.roll(middle, -1, 2) + jnp.roll(middle, 1, 2)  36.5 us
    slice x18, local copies, waits for them, and re-layouts, stencil(): beside = beside + jnp.roll(middle, -1, 3) + jnp.roll(middle, 1, 3)  24.2 us
    concatenate x9, other arithmetic, padded(): jnp.concatenate([lax.ppermute(tail, axis, [(i, (i + 1) % count) for i in...  24 us
    all_to_all x1, waiting for transfers between devices, body(): lax.all_to_all(applied_local, 'band', split_axis=1, concat_axis=0, tiled=...  23.8 us
    unnamed x49, local copies, waits for them, and re-layouts  19.1 us
  transfers between devices with their start and end apart: 22, of which 19 were waited for; matrix products, arithmetic and copies ran while one was open for 6% of the time, Pallas kernels for 0%

commit v1 on v0

--- a/solution.py
+++ b/solution.py
@@ -70,7 +70,7 @@
         lax.dot_general(point_filt, point_applied, contract, preferred_element_type=jnp.float32)
         * cell_volume
     )
-    return lax.psum((correlation_part, hamil_part), ("band", "dom"))
+    return lax.psum(lax.psum((correlation_part, hamil_part), "dom"), "band")
 
 
 def body(orbitals, potential, bounds):

time: 636 us -> 659 us (1.036)
  waiting for transfers between devices: 273 us -> 297 us
    psum x1 -> x2, waiting for transfers between devices: 134 us -> 157 us  [gram_pair(): return lax.psum(lax.psum((correlation_part, hamil_part), 'dom'), 'band')]
  transfers between devices with their start and end apart: 22 -> 23, of which waited for: 19 -> 20; matrix products, arithmetic and copies ran while one was open for 6% -> 6% of each run, Pallas kernels for 0% -> 0%
where the time goes in v1:
time: 659 us; the launch traced here: 650 us
  waiting for transfers between devices  297 us (45%)
  other arithmetic  129 us (20%)
  local copies, waits for them, and re-layouts  118 us (18%)
  matrix products  54.9 us (8%)
  starting transfers between devices  32.2 us (5%)
  between operations  18.6 us (3%)
    psum x2, waiting for transfers between devices, gram_pair(): return lax.psum(lax.psum((correlation_part, hamil_part), 'dom'), 'band')  157 us
    ppermute x9, waiting for transfers between devices, padded(): lax.ppermute(head, axis, [((i + 1) % count, i) for i in range(count)])  88.6 us
    add x8, other arithmetic, stencil(): return -0.5 * (beside - 6.0 * middle) + pot_planes * middle  72.5 us
    slice x18, local copies, waits for them, and re-layouts, stencil(): beside = beside + jnp.roll(middle, -1, 2) + jnp.roll(middle, 1, 2)  36.6 us
    all_to_all x1, waiting for transfers between devices, body(): lax.all_to_all(applied_local, 'band', split_axis=1, concat_axis=0, tiled=...  24.2 us
    slice x18, local copies, waits for them, and re-layouts, stencil(): beside = beside + jnp.roll(middle, -1, 3) + jnp.roll(middle, 1, 3)  24.2 us
    concatenate x9, other arithmetic, padded(): jnp.concatenate([lax.ppermute(tail, axis, [(i, (i + 1) % count) for i in...  24 us
    all_to_all x1, waiting for transfers between devices, body(): lax.all_to_all(point_rotated, 'band', split_axis=0, concat_axis=1, tiled=...  19.9 us
  transfers between devices with their start and end apart: 23, of which 20 were waited for; matrix products, arithmetic and copies ran while one was open for 6% of the time, Pallas kernels for 0%

profile of v1, /device:TPU:0, one launch (start us, length us, event | category | flops | bytes accessed | tf_op | source)
XLA Modules:
  0.0 649.6 jit_solution(16097058663548654766)
XLA Ops:
  22.6 4.9 collective-permute-done.1
  39.3 5.6 fusion.63
  53.6 11.0 %collective-permute-done.3 = f32[64,1,2048]{2,0,1:T(8,128)} collective-permute-done((f32[64,1,2048]{2,0,1:T(8,128)}, f32[64,1,2048]{2,0,1:T(8,128)}, u32[]{:S(2)}, u32[]{:S(2)}) %collective-permute-start.3) | collective-permute-done | bytes 524320 | tf_op jit(solution)/shard_map/ppermute | solution.py:22
  77.3 7.8 %fusion.56 = f32[64,4,64,32]{0,3,2,1:T(8,128)} fusion(f32[64,6,64,32]{0,3,2,1:T(8,128)S(1)} %bitcast.143, f32[64,4,1,32]{0,3,2,1:T(8,128)S(1)} %get-tuple-element.69, f32[64,4,63,32]{0,3,2,1:T(8,128)} %get-tuple-element.71, f32[64,4,63,32]{0,3,2,1:T(8,128)} %get-tuple-element.70, f32[64,4,1,32]{0,3,2,1:T(8,128)S(1)} %get-tuple-element.68, ...), kind=kLoop, calls=%fused_computation.73 | loop fusion | flops 7340032 | bytes 16809984 | tf_op jit(solution)/shard_map/add | solution.py:42
  93.6 11.2 %collective-permute-done.5 = f32[64,1,2048]{2,0,1:T(8,128)S(1)} collective-permute-done((f32[64,1,2048]{2,0,1:T(8,128)S(1)}, f32[64,1,2048]{2,0,1:T(8,128)S(1)}, u32[]{:S(2)}, u32[]{:S(2)}) %collective-permute-start.5) | collective-permute-done | bytes 524320 | tf_op jit(solution)/shard_map/ppermute | solution.py:22
  108.4 4.4 fusion.117
  115.8 9.8 %fusion.49 = f32[64,4,64,32]{0,3,2,1:T(8,128)} fusion(f32[64,6,64,32]{0,3,2,1:T(8,128)S(1)} %bitcast.148, f32[64,4,1,32]{0,3,2,1:T(8,128)S(1)} %get-tuple-element.61, f32[64,4,63,32]{0,3,2,1:T(8,128)} %get-tuple-element.63, f32[64,4,63,32]{0,3,2,1:T(8,128)} %get-tuple-element.62, f32[64,4,1,32]{0,3,2,1:T(8,128)S(1)} %get-tuple-element.60, ...), kind=kLoop, calls=%fused_computation.65 | loop fusion | flops 7340032 | bytes 16809984 | tf_op jit(solution)/shard_map/add | solution.py:42
  133.5 11.4 %collective-permute-done.7 = f32[64,1,2048]{2,0,1:T(8,128)S(1)} collective-permute-done((f32[64,1,2048]{2,0,1:T(8,128)S(1)}, f32[64,1,2048]{2,0,1:T(8,128)S(1)}, u32[]{:S(2)}, u32[]{:S(2)}) %collective-permute-start.7) | collective-permute-done | bytes 524320 | tf_op jit(solution)/shard_map/ppermute | solution.py:22
  156.2 9.8 %fusion.42 = f32[64,4,64,32]{0,3,2,1:T(8,128)} fusion(f32[64,6,64,32]{0,3,2,1:T(8,128)S(1)} %bitcast.153, f32[64,4,1,32]{0,3,2,1:T(8,128)S(1)} %get-tuple-element.53, f32[64,4,63,32]{0,3,2,1:T(8,128)} %get-tuple-element.55, f32[64,4,63,32]{0,3,2,1:T(8,128)} %get-tuple-element.54, f32[64,4,1,32]{0,3,2,1:T(8,128)S(1)} %get-tuple-element.52, ...), kind=kLoop, calls=%fused_computation.57 | loop fusion | flops 7340032 | bytes 16809984 | tf_op jit(solution)/shard_map/add | solution.py:42
  174.0 11.5 %collective-permute-done.9 = f32[64,1,2048]{2,0,1:T(8,128)S(1)} collective-permute-done((f32[64,1,2048]{2,0,1:T(8,128)S(1)}, f32[64,1,2048]{2,0,1:T(8,128)S(1)}, u32[]{:S(2)}, u32[]{:S(2)}) %collective-permute-start.9) | collective-permute-done | bytes 524320 | tf_op jit(solution)/shard_map/ppermute | solution.py:22
  196.5 9.8 %fusion.35 = f32[64,4,64,32]{0,3,2,1:T(8,128)} fusion(f32[64,6,64,32]{0,3,2,1:T(8,128)S(1)} %bitcast.158, f32[64,4,1,32]{0,3,2,1:T(8,128)S(1)} %get-tuple-element.45, f32[64,4,63,32]{0,3,2,1:T(8,128)} %get-tuple-element.47, f32[64,4,63,32]{0,3,2,1:T(8,128)} %get-tuple-element.46, f32[64,4,1,32]{0,3,2,1:T(8,128)S(1)} %get-tuple-element.44, ...), kind=kLoop, calls=%fused_computation.49 | loop fusion | flops 7340032 | bytes 16809984 | tf_op jit(solution)/shard_map/add | solution.py:42
  214.4 11.7 %collective-permute-done.11 = f32[64,1,2048]{2,0,1:T(8,128)S(1)} collective-permute-done((f32[64,1,2048]{2,0,1:T(8,128)S(1)}, f32[64,1,2048]{2,0,1:T(8,128)S(1)}, u32[]{:S(2)}, u32[]{:S(2)}) %collective-permute-start.11) | collective-permute-done | bytes 524320 | tf_op jit(solution)/shard_map/ppermute | solution.py:22
  237.4 9.8 %fusion.28 = f32[64,4,64,32]{0,3,2,1:T(8,128)} fusion(f32[64,6,64,32]{0,3,2,1:T(8,128)S(1)} %bitcast.163, f32[64,4,1,32]{0,3,2,1:T(8,128)S(1)} %get-tuple-element.37, f32[64,4,63,32]{0,3,2,1:T(8,128)} %get-tuple-element.39, f32[64,4,63,32]{0,3,2,1:T(8,128)} %get-tuple-element.38, f32[64,4,1,32]{0,3,2,1:T(8,128)S(1)} %get-tuple-element.36, ...), kind=kLoop, calls=%fused_computation.41 | loop fusion | flops 7340032 | bytes 16809984 | tf_op jit(solution)/shard_map/add | solution.py:42
  255.0 11.7 %collective-permute-done.13 = f32[64,1,2048]{2,0,1:T(8,128)S(1)} collective-permute-done((f32[64,1,2048]{2,0,1:T(8,128)S(1)}, f32[64,1,2048]{2,0,1:T(8,128)S(1)}, u32[]{:S(2)}, u32[]{:S(2)}) %collective-permute-start.13) | collective-permute-done | bytes 524320 | tf_op jit(solution)/shard_map/ppermute | solution.py:22
  277.8 9.8 %fusion.21 = f32[64,4,64,32]{0,3,2,1:T(8,128)} fusion(f32[64,6,64,32]{0,3,2,1:T(8,128)S(1)} %bitcast.168, f32[64,4,1,32]{0,3,2,1:T(8,128)S(1)} %get-tuple-element.29, f32[64,4,63,32]{0,3,2,1:T(8,128)} %get-tuple-element.31, f32[64,4,63,32]{0,3,2,1:T(8,128)} %get-tuple-element.30, f32[64,4,1,32]{0,3,2,1:T(8,128)S(1)} %get-tuple-element.28, ...), kind=kLoop, calls=%fused_computation.33 | loop fusion | flops 7340032 | bytes 16809984 | tf_op jit(solution)/shard_map/add | solution.py:42
  295.6 11.7 %collective-permute-done.15 = f32[64,1,2048]{2,0,1:T(8,128)S(1)} collective-permute-done((f32[64,1,2048]{2,0,1:T(8,128)S(1)}, f32[64,1,2048]{2,0,1:T(8,128)S(1)}, u32[]{:S(2)}, u32[]{:S(2)}) %collective-permute-start.15) | collective-permute-done | bytes 524320 | tf_op jit(solution)/shard_map/ppermute | solution.py:22
  318.5 9.8 %fusion.14 = f32[64,4,64,32]{0,3,2,1:T(8,128)} fusion(f32[64,6,64,32]{0,3,2,1:T(8,128)S(1)} %bitcast.173, f32[64,4,1,32]{0,3,2,1:T(8,128)S(1)} %get-tuple-element.21, f32[64,4,63,32]{0,3,2,1:T(8,128)} %get-tuple-element.23, f32[64,4,63,32]{0,3,2,1:T(8,128)} %get-tuple-element.22, f32[64,4,1,32]{0,3,2,1:T(8,128)S(1)} %get-tuple-element.20, ...), kind=kLoop, calls=%fused_computation.25 | loop fusion | flops 7340032 | bytes 16809984 | tf_op jit(solution)/shard_map/add | solution.py:42
  341.4 5.8 all-to-all-start
  360.7 5.6 fusion.7
  367.9 5.3 all-to-all-done
  378.6 24.2 %all-to-all-done.2 = bf16[64,8,1024]{2,0,1:T(8,128)(2,1)S(1)} async-done(((bf16[64,8,1024]{2,0,1:T(8,128)(2,1)}), bf16[64,8,1024]{2,0,1:T(8,128)(2,1)S(1)}, u32[]{:S(2)}, u32[]{:S(2)}) %all-to-all-start.2) | async-done | bytes 1048608 | tf_op jit(solution)/shard_map/all_to_all | solution.py:92
  405.0 50.6 %all-reduce.7.cloned.1.call-done = (f32[512,512]{1,0:T(8,128)}, f32[512,512]{1,0:T(8,128)}) async-done(((f32[512,512]{1,0:T(8,128)}, f32[512,512]{1,0:T(8,128)}), (f32[512,512]{1,0:T(8,128)}, f32[512,512]{1,0:T(8,128)})) %all-reduce.7.cloned.1.call-update) | async-done | bytes 2097168 | tf_op jit(solution)/shard_map/psum | solution.py:73
  455.7 106.1 %all-reduce.5.cloned.1.call-done = (f32[512,512]{1,0:T(8,128)}, f32[512,512]{1,0:T(8,128)}) async-done(((f32[512,512]{1,0:T(8,128)}, f32[512,512]{1,0:T(8,128)}), (f32[512,512]{1,0:T(8,128)}, f32[512,512]{1,0:T(8,128)})) %all-reduce.5.cloned.1.call-update) | async-done | bytes 2097168 | tf_op jit(solution)/shard_map/psum | solution.py:73
  620.3 19.9 %all-to-all-done.1 = bf16[8,64,1024]{2,1,0:T(8,128)(2,1)S(1)} async-done(((bf16[8,64,1024]{2,1,0:T(8,128)(2,1)}), bf16[8,64,1024]{2,1,0:T(8,128)(2,1)S(1)}, u32[]{:S(2)}, u32[]{:S(2)}) %all-to-all-start.1) | async-done | bytes 1048608 | tf_op jit(solution)/shard_map/all_to_all | solution.py:109
  (216 shorter events, 251.6 us)
Async XLA Ops:
  13.5 14.0 %collective-permute-start.1 = (f32[64,1,2048]{2,0,1:T(8,128)}, f32[64,1,2048]{2,0,1:T(8,128)}, u32[]{:S(2)}, u32[]{:S(2)}) collective-permute-start(f32[64,1,2048]{2,0,1:T(8,128)} %copy.12), channel_id=1, source_target_pairs={{1,0},{2,1},{3,2},{0,3},{5,4},{6,5},{7,6},{4,7},{9,8},{10,9},{11,1... | collective-permute-start | bytes 1572872 | tf_op jit(solution)/shard_map/ppermute | solution.py:22
  17.1 12.5 %collective-permute-start = (f32[64,1,2048]{2,0,1:T(8,128)}, f32[64,1,2048]{2,0,1:T(8,128)}, u32[]{:S(2)}, u32[]{:S(2)}) collective-permute-start(f32[64,1,2048]{2,0,1:T(8,128)} %copy.11), channel_id=1, source_target_pairs={{0,1},{1,2},{2,3},{3,0},{4,5},{5,6},{6,7},{7,4},{8,9},{9,10},{10,1... | collective-permute-start | bytes 1572872 | tf_op jit(solution)/shard_map/ppermute | solution.py:20
  51.0 13.6 %collective-permute-start.3 = (f32[64,1,2048]{2,0,1:T(8,128)}, f32[64,1,2048]{2,0,1:T(8,128)}, u32[]{:S(2)}, u32[]{:S(2)}) collective-permute-start(f32[64,1,2048]{2,0,1:T(8,128)} %copy.16), channel_id=1, source_target_pairs={{1,0},{2,1},{3,2},{0,3},{5,4},{6,5},{7,6},{4,7},{9,8},{10,9},{11,1... | collective-permute-start | bytes 1572872 | tf_op jit(solution)/shard_map/ppermute | solution.py:22
  53.6 12.4 %collective-permute-start.2 = (f32[64,1,2048]{2,0,1:T(8,128)}, f32[64,1,2048]{2,0,1:T(8,128)}, u32[]{:S(2)}, u32[]{:S(2)}) collective-permute-start(f32[64,1,2048]{2,0,1:T(8,128)} %copy.15), channel_id=1, source_target_pairs={{0,1},{1,2},{2,3},{3,0},{4,5},{5,6},{6,7},{7,4},{8,9},{9,10},{10,1... | collective-permute-start | bytes 1572872 | tf_op jit(solution)/shard_map/ppermute | solution.py:20
  90.8 14.0 %collective-permute-start.5 = (f32[64,1,2048]{2,0,1:T(8,128)S(1)}, f32[64,1,2048]{2,0,1:T(8,128)S(1)}, u32[]{:S(2)}, u32[]{:S(2)}) collective-permute-start(f32[64,1,2048]{2,0,1:T(8,128)S(1)} %copy.20), channel_id=1, source_target_pairs={{1,0},{2,1},{3,2},{0,3},{5,4},{6,5},{7,6},{4,7},{9,8},{10,9},{11,1... | collective-permute-start | bytes 1572872 | tf_op jit(solution)/shard_map/ppermute | solution.py:22
  93.4 11.9 %collective-permute-start.4 = (f32[64,1,2048]{2,0,1:T(8,128)S(1)}, f32[64,1,2048]{2,0,1:T(8,128)S(1)}, u32[]{:S(2)}, u32[]{:S(2)}) collective-permute-start(f32[64,1,2048]{2,0,1:T(8,128)S(1)} %copy.19), channel_id=1, source_target_pairs={{0,1},{1,2},{2,3},{3,0},{4,5},{5,6},{6,7},{7,4},{8,9},{9,10},{10,1... | collective-permute-start | bytes 1572872 | tf_op jit(solution)/shard_map/ppermute | solution.py:20
  131.3 13.7 %collective-permute-start.7 = (f32[64,1,2048]{2,0,1:T(8,128)S(1)}, f32[64,1,2048]{2,0,1:T(8,128)S(1)}, u32[]{:S(2)}, u32[]{:S(2)}) collective-permute-start(f32[64,1,2048]{2,0,1:T(8,128)S(1)} %copy.24), channel_id=1, source_target_pairs={{1,0},{2,1},{3,2},{0,3},{5,4},{6,5},{7,6},{4,7},{9,8},{10,9},{11,1... | collective-permute-start | bytes 1572872 | tf_op jit(solution)/shard_map/ppermute | solution.py:22
  133.4 12.1 %collective-permute-start.6 = (f32[64,1,2048]{2,0,1:T(8,128)S(1)}, f32[64,1,2048]{2,0,1:T(8,128)S(1)}, u32[]{:S(2)}, u32[]{:S(2)}) collective-permute-start(f32[64,1,2048]{2,0,1:T(8,128)S(1)} %copy.23), channel_id=1, source_target_pairs={{0,1},{1,2},{2,3},{3,0},{4,5},{5,6},{6,7},{7,4},{8,9},{9,10},{10,1... | collective-permute-start | bytes 1572872 | tf_op jit(solution)/shard_map/ppermute | solution.py:20
  171.6 13.9 %collective-permute-start.9 = (f32[64,1,2048]{2,0,1:T(8,128)S(1)}, f32[64,1,2048]{2,0,1:T(8,128)S(1)}, u32[]{:S(2)}, u32[]{:S(2)}) collective-permute-start(f32[64,1,2048]{2,0,1:T(8,128)S(1)} %copy.28), channel_id=1, source_target_pairs={{1,0},{2,1},{3,2},{0,3},{5,4},{6,5},{7,6},{4,7},{9,8},{10,9},{11,1... | collective-permute-start | bytes 1572872 | tf_op jit(solution)/shard_map/ppermute | solution.py:22
  173.6 12.3 %collective-permute-start.8 = (f32[64,1,2048]{2,0,1:T(8,128)S(1)}, f32[64,1,2048]{2,0,1:T(8,128)S(1)}, u32[]{:S(2)}, u32[]{:S(2)}) collective-permute-start(f32[64,1,2048]{2,0,1:T(8,128)S(1)} %copy.27), channel_id=1, source_target_pairs={{0,1},{1,2},{2,3},{3,0},{4,5},{5,6},{6,7},{7,4},{8,9},{9,10},{10,1... | collective-permute-start | bytes 1572872 | tf_op jit(solution)/shard_map/ppermute | solution.py:20
  211.9 14.2 %collective-permute-start.11 = (f32[64,1,2048]{2,0,1:T(8,128)S(1)}, f32[64,1,2048]{2,0,1:T(8,128)S(1)}, u32[]{:S(2)}, u32[]{:S(2)}) collective-permute-start(f32[64,1,2048]{2,0,1:T(8,128)S(1)} %copy.32), channel_id=1, source_target_pairs={{1,0},{2,1},{3,2},{0,3},{5,4},{6,5},{7,6},{4,7},{9,8},{10,9},{11,1... | collective-permute-start | bytes 1572872 | tf_op jit(solution)/shard_map/ppermute | solution.py:22
  214.4 12.4 %collective-permute-start.10 = (f32[64,1,2048]{2,0,1:T(8,128)S(1)}, f32[64,1,2048]{2,0,1:T(8,128)S(1)}, u32[]{:S(2)}, u32[]{:S(2)}) collective-permute-start(f32[64,1,2048]{2,0,1:T(8,128)S(1)} %copy.31), channel_id=1, source_target_pairs={{0,1},{1,2},{2,3},{3,0},{4,5},{5,6},{6,7},{7,4},{8,9},{9,10},{10,1... | collective-permute-start | bytes 1572872 | tf_op jit(solution)/shard_map/ppermute | solution.py:20
  252.8 13.9 %collective-permute-start.13 = (f32[64,1,2048]{2,0,1:T(8,128)S(1)}, f32[64,1,2048]{2,0,1:T(8,128)S(1)}, u32[]{:S(2)}, u32[]{:S(2)}) collective-permute-start(f32[64,1,2048]{2,0,1:T(8,128)S(1)} %copy.36), channel_id=1, source_target_pairs={{1,0},{2,1},{3,2},{0,3},{5,4},{6,5},{7,6},{4,7},{9,8},{10,9},{11,1... | collective-permute-start | bytes 1572872 | tf_op jit(solution)/shard_map/ppermute | solution.py:22
  254.8 12.4 %collective-permute-start.12 = (f32[64,1,2048]{2,0,1:T(8,128)S(1)}, f32[64,1,2048]{2,0,1:T(8,128)S(1)}, u32[]{:S(2)}, u32[]{:S(2)}) collective-permute-start(f32[64,1,2048]{2,0,1:T(8,128)S(1)} %copy.35), channel_id=1, source_target_pairs={{0,1},{1,2},{2,3},{3,0},{4,5},{5,6},{6,7},{7,4},{8,9},{9,10},{10,1... | collective-permute-start | bytes 1572872 | tf_op jit(solution)/shard_map/ppermute | solution.py:20
  293.2 14.1 %collective-permute-start.15 = (f32[64,1,2048]{2,0,1:T(8,128)S(1)}, f32[64,1,2048]{2,0,1:T(8,128)S(1)}, u32[]{:S(2)}, u32[]{:S(2)}) collective-permute-start(f32[64,1,2048]{2,0,1:T(8,128)S(1)} %copy.40), channel_id=1, source_target_pairs={{1,0},{2,1},{3,2},{0,3},{5,4},{6,5},{7,6},{4,7},{9,8},{10,9},{11,1... | collective-permute-start | bytes 1572872 | tf_op jit(solution)/shard_map/ppermute | solution.py:22
  295.5 12.4 %collective-permute-start.14 = (f32[64,1,2048]{2,0,1:T(8,128)S(1)}, f32[64,1,2048]{2,0,1:T(8,128)S(1)}, u32[]{:S(2)}, u32[]{:S(2)}) collective-permute-start(f32[64,1,2048]{2,0,1:T(8,128)S(1)} %copy.39), channel_id=1, source_target_pairs={{0,1},{1,2},{2,3},{3,0},{4,5},{5,6},{6,7},{7,4},{8,9},{9,10},{10,1... | collective-permute-start | bytes 1572872 | tf_op jit(solution)/shard_map/ppermute | solution.py:20
  318.5 9.9 %copy-start.19 = (f32[64,4,2048]{0,2,1:T(8,128)S(1)}, f32[64,4,2048]{0,2,1:T(8,128)}, u32[]{:S(2)}) copy-start(f32[64,4,2048]{0,2,1:T(8,128)} %copy-done.18) | copy-start | bytes 6291460
  337.1 13.8 %collective-permute-start.17 = (f32[64,1,2048]{2,0,1:T(8,128)}, f32[64,1,2048]{2,0,1:T(8,128)}, u32[]{:S(2)}, u32[]{:S(2)}) collective-permute-start(f32[64,1,2048]{2,0,1:T(8,128)} %copy.46), channel_id=1, source_target_pairs={{1,0},{2,1},{3,2},{0,3},{5,4},{6,5},{7,6},{4,7},{9,8},{10,9},{11,1... | collective-permute-start | bytes 1572872 | tf_op jit(solution)/shard_map/ppermute | solution.py:22
  339.8 12.4 %collective-permute-start.16 = (f32[64,1,2048]{2,0,1:T(8,128)}, f32[64,1,2048]{2,0,1:T(8,128)}, u32[]{:S(2)}, u32[]{:S(2)}) collective-permute-start(f32[64,1,2048]{2,0,1:T(8,128)} %copy.45), channel_id=1, source_target_pairs={{0,1},{1,2},{2,3},{3,0},{4,5},{5,6},{6,7},{7,4},{8,9},{9,10},{10,1... | collective-permute-start | bytes 1572872 | tf_op jit(solution)/shard_map/ppermute | solution.py:20
  341.4 31.8 %all-to-all-start = ((bf16[64,8,1024]{2,0,1:T(8,128)(2,1)}), bf16[64,8,1024]{2,0,1:T(8,128)(2,1)S(1)}, u32[]{:S(2)}, u32[]{:S(2)}) async-start(bf16[64,8,1024]{2,0,1:T(8,128)(2,1)} %copy.43), calls=%async_computation | async-start | bytes 2097152 | tf_op jit(solution)/shard_map/all_to_all | solution.py:91
  373.2 29.6 %all-to-all-start.2 = ((bf16[64,8,1024]{2,0,1:T(8,128)(2,1)}), bf16[64,8,1024]{2,0,1:T(8,128)(2,1)S(1)}, u32[]{:S(2)}, u32[]{:S(2)}) async-start(bf16[64,8,1024]{2,0,1:T(8,128)(2,1)} %copy.49), calls=%async_computation.2 | async-start | bytes 2097152 | tf_op jit(solution)/shard_map/all_to_all | solution.py:92
  376.9 78.8 %all-reduce.7.cloned.1.call-start = ((), (), s32[]{:S(2)}) async-start(), calls=%async_computation.4 | async-start | bytes 4194304 | tf_op jit(solution)/shard_map/psum | solution.py:73
  404.6 157.2 %all-reduce.5.cloned.1.call-start = ((), (), s32[]{:S(2)}) async-start(), calls=%async_computation.3 | async-start | bytes 4194304 | tf_op jit(solution)/shard_map/psum | solution.py:73
  610.5 29.7 %all-to-all-start.1 = ((bf16[8,64,1024]{2,1,0:T(8,128)(2,1)}), bf16[8,64,1024]{2,1,0:T(8,128)(2,1)S(1)}, u32[]{:S(2)}, u32[]{:S(2)}) async-start(bf16[8,64,1024]{2,1,0:T(8,128)(2,1)} %bitcast.21), calls=%async_computation.1 | async-start | bytes 2097152 | tf_op jit(solution)/shard_map/all_to_all | solution.py:109
  (23 other events, 153.7 us)
Sparse Core Ops, SparseCore 0:
  404.7 50.9 all-reduce.6
  459.3 102.3 all-reduce.4
